TPU v7x, 32 devices: a whole 2x2x4 slice. The times are simulated.
32 devices in a mesh: group: 2 (over x), ctx: 16 (over z, y, core).
Axes of the slice: x: 2, y: 2, z: 4, core: 2. Of those that a mesh axis runs over, the one named last changes fastest.
Arguments:
- query_rows: bfloat16 [4096, 4096], P(('group', 'ctx')), parts along dimension 0, may hold values from -6 to 6
- key_rows: bfloat16 [4096, 4096], P(('group', 'ctx')), parts along dimension 0, may hold values from -6 to 6
- value_rows: bfloat16 [4096, 4096], P(('group', 'ctx')), parts along dimension 0, may hold values from -6 to 6
- conv_taps: float32 [3, 3, 4096], replicated, may hold values from -3.5 to 3.5
- decay_rate: float32 [4096], replicated, may hold values from 0.0007324219 to 0.034
- lag_profile: float32 [2048], replicated, may hold values from -3.6681164 to 3.6681164
- skip_gain: float32 [4096], replicated, may hold values from 0.5 to 1.5
- pair_lists: int32 [32, 9, 2], P('group'), parts along dimension 0, may hold values from -1 to 15, as said below
Outputs:
- layer_out: bfloat16 [4096, 4096], P(('group', 'ctx')), parts along dimension 0
There are 2 independent parts, one for each index of `group`. A program takes and returns all parts, laid end to end along the dimension named above; an argument that names none is the same for every part. Nothing has to cross between parts.
Inputs may be any that keep to these rules, and one draw needn't show every extreme that they name: `pair_lists`: row r lists the pairs that reader r handles. Every live pair (source span <= target span, both in the same document) appears exactly once over all rows, and no other pair appears. A reader's sources are r or 15 - r, its targets are distinct, and unused entries are (-1, -1) after the used ones; some reader's row is full. The sequence holds two documents, the second beginning at a span between 4 and 12.
All inputs are finite; a program needn't handle non-finite values.
Results may differ from a plain program's by a relative error of at most 0.0051.
Values may be sent and summed in bfloat16 or wider, within the bound.
A program may use at most 128 MiB of HBM per device.

v0:
```python
import jax
import jax.numpy as jnp
from jax import lax
from jax.sharding import PartitionSpec as P


def from_behind(value, axis, steps):
    count = lax.axis_size(axis)
    leading, last = (max(0, -steps), min(count, count - steps))
    return lax.ppermute(value, axis, [(source, source + steps) for source in range(leading, last)])


def short_conv(extended, conv_taps, span_rows):
    values = extended.astype(jnp.float32)
    return (
        conv_taps[0] * values[2:]
        + conv_taps[1] * values[1 : span_rows + 1]
        + conv_taps[2] * values[:span_rows]
    )


def toeplitz_of(window, span_rows):
    reverse_win = window[::-1]
    extended = jnp.concatenate([reverse_win, jnp.zeros((1,), reverse_win.dtype)])
    tiled = jnp.tile(extended, span_rows + 1)
    start = span_rows - 1
    flat_part = tiled[start : start + span_rows * (2 * span_rows - 1)]
    return flat_part.reshape(span_rows, 2 * span_rows - 1)[:, :span_rows]


def block_term(source, span_gap, decay_rate, padded_lag, span_rows):
    gap_rows = span_gap * span_rows
    window = lax.dynamic_slice_in_dim(padded_lag, gap_rows + 1, 2 * span_rows - 1)
    toeplitz = toeplitz_of(window, span_rows)
    positions = jnp.arange(span_rows, dtype=jnp.float32)
    scaled = source.astype(jnp.float32) * jnp.exp(decay_rate[None, :] * positions[:, None])
    mixed = jnp.dot(
        toeplitz, scaled, precision=lax.Precision.HIGHEST, preferred_element_type=jnp.float32
    )
    distance = positions[:, None] + gap_rows.astype(jnp.float32)
    return (mixed * jnp.exp(-decay_rate[None, :] * distance)).astype(jnp.bfloat16)


def on_device(
    query_rows, key_rows, value_rows, conv_taps, decay_rate, lag_profile, skip_gain, pair_lists
):
    span_rows, channels = query_rows.shape
    ctx_count = lax.axis_size("ctx")
    own_index = lax.axis_index("ctx")
    rims = jnp.stack(
        [query_rows[span_rows - 2 :], key_rows[span_rows - 2 :], value_rows[span_rows - 2 :]]
    )
    before = from_behind(rims, "ctx", 1)
    query_feat = short_conv(
        jnp.concatenate([before[0], query_rows], axis=0), conv_taps[0], span_rows
    )
    key_feat = short_conv(jnp.concatenate([before[1], key_rows], axis=0), conv_taps[1], span_rows)
    value_feat = short_conv(
        jnp.concatenate([before[2], value_rows], axis=0), conv_taps[2], span_rows
    )
    gated = (key_feat * value_feat).astype(jnp.bfloat16)
    padded_lag = jnp.concatenate([jnp.zeros((span_rows,), jnp.float32), lag_profile])
    sources = pair_lists[:, :, 0].reshape(-1)
    targets = pair_lists[:, :, 1].reshape(-1)
    span_ids = jnp.arange(ctx_count, dtype=jnp.int32)
    live_from = jnp.any(
        (sources[:, None] == span_ids[None, :]) & (targets[:, None] == own_index), axis=0
    )
    running = jnp.zeros((span_rows, channels), jnp.float32)
    pieces = lax.all_gather(gated, "ctx", axis=0, tiled=True).reshape(-1, span_rows, channels)

    def add_span(carried, element):
        offset, source = element

        def compute_block():
            return block_term(source, own_index - offset, decay_rate, padded_lag, span_rows).astype(
                jnp.float32
            )

        def zero_block():
            return jnp.zeros((span_rows, channels), jnp.float32)

        return (carried + lax.cond(live_from[offset], compute_block, zero_block), None)

    running, unused = lax.scan(
        add_span, running, (jnp.arange(pieces.shape[0], dtype=jnp.int32), pieces)
    )
    layer_out = (query_feat * (running + skip_gain[None, :] * gated.astype(jnp.float32))).astype(
        jnp.bfloat16
    )
    return layer_out


def solution(mesh):
    return jax.shard_map(
        on_device,
        mesh=mesh,
        in_specs=(
            P(("group", "ctx"), None),
            P(("group", "ctx"), None),
            P(("group", "ctx"), None),
            P(),
            P(),
            P(),
            P(),
            P("group", None, None),
        ),
        out_specs=P(("group", "ctx"), None),
        check_vma=False,
    )
```

profile of v0, /device:TPU:29, one launch (start us, length us, event | category | flops | bytes accessed | tf_op | source)
XLA Modules:
  0.0 315.1 jit_solution(14223690343918682168)
XLA Ops:
  6.5 0.9 slice_bitcast_fusion.5
  7.5 0.9 slice_bitcast_fusion.3
  8.5 1.3 collective-permute-start
  9.8 1.2 fusion.22
  11.8 1.5 maximum_convert_fusion.1
  13.7 2.3 fusion.12
  16.6 1.7 maximum_convert_fusion
  18.3 125.3 %all-gather.2.cloned.1.call-done = bf16[2048,4096]{1,0:T(8,128)(2,1)} async-done(((bf16[128,4096]{1,0:T(8,128)(2,1)}), bf16[2048,4096]{1,0:T(8,128)(2,1)}) %all-gather.2.cloned.1.call-update) | async-done | bytes 16777232 | tf_op jit(solution)/shard_map/all_gather | solution.py:70
  143.6 159.1 %while.11 = (s32[]{:T(128)}, f32[128,4096]{1,0:T(8,128)}, s32[16]{0:T(128)S(1)}, pred[16]{0:T(512)(128)(4,1)S(1)}, s32[]{:T(128)}, /*index=5*/f32[2176]{0:T(1024...) while((s32[]{:T(128)}, f32[128,4096]{1,0:T(8,128)}, ...), condition=%wide.region_4.5_spmd.clone, body=%wide.region_1.4_spmd.clone.sunk | while | flops 810029440 | bytes 10497838 | solution.py:85
  147.3 1.5 select_add_fusion.2
  152.4 3.1 select_add_fusion.2
  159.2 3.1 select_add_fusion.2
  166.0 3.1 select_add_fusion.2
  172.7 3.1 select_add_fusion.2
  179.2 5.0 %conditional.3 = (f32[128,4096]{1,0:T(8,128)S(1)}) conditional(s32[]{:T(128)} %bitcast.38, () %tuple.46, (s32[]{:T(128)}, s32[]{:T(128)}, f32[2176]{0:T(1024)S(1)}, bf16[16,128,4096]{2,1,0:T(8,128)(2,1)}, s32[]{:T(128)}, /*index=5*/f32[4096]{0:T(1024)S(1)}) %tuple.47), branch_computations={%region_2.2_spmd, %region_3.3_spmd} | conditional | flops 808980864 | bytes 4206158 | solution.py:83
  180.6 3.6 %fusion.1 = f32[128,4096]{1,0:T(8,128)S(1)} fusion(f32[128]{0:T(128)S(1)} %iota_add_fusion, f32[4096]{0:T(1024)S(1)} %neg.4, f32[4096]{0:T(1024)S(1)} %get-tuple-element.72, bf16[16,128,4096]{2,1,0:T(8,128)(2,1)} %get-tuple-element.70, s32[]{:T(128)} %get-tuple-element.71, f32[128,255]{1,0:T(8,128)S(1)} %reshape.47), kind=kOutput, calls=%fused_computation.2 | convolution fusion | flops 808976384 | bytes 3245056 | tf_op jit(solution)/shard_map/while/body/eval_jaxpr/cond/branch_1_fun/dot_general | solution.py:37
  184.2 3.1 select_add_fusion.2
  190.8 5.0 %conditional.3 = (f32[128,4096]{1,0:T(8,128)S(1)}) conditional(s32[]{:T(128)} %bitcast.38, () %tuple.46, (s32[]{:T(128)}, s32[]{:T(128)}, f32[2176]{0:T(1024)S(1)}, bf16[16,128,4096]{2,1,0:T(8,128)(2,1)}, s32[]{:T(128)}, /*index=5*/f32[4096]{0:T(1024)S(1)}) %tuple.47), branch_computations={%region_2.2_spmd, %region_3.3_spmd} | conditional | flops 808980864 | bytes 4206158 | solution.py:83
  192.2 3.6 %fusion.1 = f32[128,4096]{1,0:T(8,128)S(1)} fusion(f32[128]{0:T(128)S(1)} %iota_add_fusion, f32[4096]{0:T(1024)S(1)} %neg.4, f32[4096]{0:T(1024)S(1)} %get-tuple-element.72, bf16[16,128,4096]{2,1,0:T(8,128)(2,1)} %get-tuple-element.70, s32[]{:T(128)} %get-tuple-element.71, f32[128,255]{1,0:T(8,128)S(1)} %reshape.47), kind=kOutput, calls=%fused_computation.2 | convolution fusion | flops 808976384 | bytes 3245056 | tf_op jit(solution)/shard_map/while/body/eval_jaxpr/cond/branch_1_fun/dot_general | solution.py:37
  195.8 3.1 select_add_fusion.2
  202.3 5.0 %conditional.3 = (f32[128,4096]{1,0:T(8,128)S(1)}) conditional(s32[]{:T(128)} %bitcast.38, () %tuple.46, (s32[]{:T(128)}, s32[]{:T(128)}, f32[2176]{0:T(1024)S(1)}, bf16[16,128,4096]{2,1,0:T(8,128)(2,1)}, s32[]{:T(128)}, /*index=5*/f32[4096]{0:T(1024)S(1)}) %tuple.47), branch_computations={%region_2.2_spmd, %region_3.3_spmd} | conditional | flops 808980864 | bytes 4206158 | solution.py:83
  203.7 3.6 %fusion.1 = f32[128,4096]{1,0:T(8,128)S(1)} fusion(f32[128]{0:T(128)S(1)} %iota_add_fusion, f32[4096]{0:T(1024)S(1)} %neg.4, f32[4096]{0:T(1024)S(1)} %get-tuple-element.72, bf16[16,128,4096]{2,1,0:T(8,128)(2,1)} %get-tuple-element.70, s32[]{:T(128)} %get-tuple-element.71, f32[128,255]{1,0:T(8,128)S(1)} %reshape.47), kind=kOutput, calls=%fused_computation.2 | convolution fusion | flops 808976384 | bytes 3245056 | tf_op jit(solution)/shard_map/while/body/eval_jaxpr/cond/branch_1_fun/dot_general | solution.py:37
  207.3 3.1 select_add_fusion.2
  213.8 5.0 %conditional.3 = (f32[128,4096]{1,0:T(8,128)S(1)}) conditional(s32[]{:T(128)} %bitcast.38, () %tuple.46, (s32[]{:T(128)}, s32[]{:T(128)}, f32[2176]{0:T(1024)S(1)}, bf16[16,128,4096]{2,1,0:T(8,128)(2,1)}, s32[]{:T(128)}, /*index=5*/f32[4096]{0:T(1024)S(1)}) %tuple.47), branch_computations={%region_2.2_spmd, %region_3.3_spmd} | conditional | flops 808980864 | bytes 4206158 | solution.py:83
  215.3 3.6 %fusion.1 = f32[128,4096]{1,0:T(8,128)S(1)} fusion(f32[128]{0:T(128)S(1)} %iota_add_fusion, f32[4096]{0:T(1024)S(1)} %neg.4, f32[4096]{0:T(1024)S(1)} %get-tuple-element.72, bf16[16,128,4096]{2,1,0:T(8,128)(2,1)} %get-tuple-element.70, s32[]{:T(128)} %get-tuple-element.71, f32[128,255]{1,0:T(8,128)S(1)} %reshape.47), kind=kOutput, calls=%fused_computation.2 | convolution fusion | flops 808976384 | bytes 3245056 | tf_op jit(solution)/shard_map/while/body/eval_jaxpr/cond/branch_1_fun/dot_general | solution.py:37
  218.9 3.1 select_add_fusion.2
  225.4 5.0 %conditional.3 = (f32[128,4096]{1,0:T(8,128)S(1)}) conditional(s32[]{:T(128)} %bitcast.38, () %tuple.46, (s32[]{:T(128)}, s32[]{:T(128)}, f32[2176]{0:T(1024)S(1)}, bf16[16,128,4096]{2,1,0:T(8,128)(2,1)}, s32[]{:T(128)}, /*index=5*/f32[4096]{0:T(1024)S(1)}) %tuple.47), branch_computations={%region_2.2_spmd, %region_3.3_spmd} | conditional | flops 808980864 | bytes 4206158 | solution.py:83
  226.8 3.6 %fusion.1 = f32[128,4096]{1,0:T(8,128)S(1)} fusion(f32[128]{0:T(128)S(1)} %iota_add_fusion, f32[4096]{0:T(1024)S(1)} %neg.4, f32[4096]{0:T(1024)S(1)} %get-tuple-element.72, bf16[16,128,4096]{2,1,0:T(8,128)(2,1)} %get-tuple-element.70, s32[]{:T(128)} %get-tuple-element.71, f32[128,255]{1,0:T(8,128)S(1)} %reshape.47), kind=kOutput, calls=%fused_computation.2 | convolution fusion | flops 808976384 | bytes 3245056 | tf_op jit(solution)/shard_map/while/body/eval_jaxpr/cond/branch_1_fun/dot_general | solution.py:37
  230.4 3.1 select_add_fusion.2
  236.9 5.0 %conditional.3 = (f32[128,4096]{1,0:T(8,128)S(1)}) conditional(s32[]{:T(128)} %bitcast.38, () %tuple.46, (s32[]{:T(128)}, s32[]{:T(128)}, f32[2176]{0:T(1024)S(1)}, bf16[16,128,4096]{2,1,0:T(8,128)(2,1)}, s32[]{:T(128)}, /*index=5*/f32[4096]{0:T(1024)S(1)}) %tuple.47), branch_computations={%region_2.2_spmd, %region_3.3_spmd} | conditional | flops 808980864 | bytes 4206158 | solution.py:83
  238.3 3.6 %fusion.1 = f32[128,4096]{1,0:T(8,128)S(1)} fusion(f32[128]{0:T(128)S(1)} %iota_add_fusion, f32[4096]{0:T(1024)S(1)} %neg.4, f32[4096]{0:T(1024)S(1)} %get-tuple-element.72, bf16[16,128,4096]{2,1,0:T(8,128)(2,1)} %get-tuple-element.70, s32[]{:T(128)} %get-tuple-element.71, f32[128,255]{1,0:T(8,128)S(1)} %reshape.47), kind=kOutput, calls=%fused_computation.2 | convolution fusion | flops 808976384 | bytes 3245056 | tf_op jit(solution)/shard_map/while/body/eval_jaxpr/cond/branch_1_fun/dot_general | solution.py:37
  241.9 3.1 select_add_fusion.2
  248.5 5.0 %conditional.3 = (f32[128,4096]{1,0:T(8,128)S(1)}) conditional(s32[]{:T(128)} %bitcast.38, () %tuple.46, (s32[]{:T(128)}, s32[]{:T(128)}, f32[2176]{0:T(1024)S(1)}, bf16[16,128,4096]{2,1,0:T(8,128)(2,1)}, s32[]{:T(128)}, /*index=5*/f32[4096]{0:T(1024)S(1)}) %tuple.47), branch_computations={%region_2.2_spmd, %region_3.3_spmd} | conditional | flops 808980864 | bytes 4206158 | solution.py:83
  249.9 3.6 %fusion.1 = f32[128,4096]{1,0:T(8,128)S(1)} fusion(f32[128]{0:T(128)S(1)} %iota_add_fusion, f32[4096]{0:T(1024)S(1)} %neg.4, f32[4096]{0:T(1024)S(1)} %get-tuple-element.72, bf16[16,128,4096]{2,1,0:T(8,128)(2,1)} %get-tuple-element.70, s32[]{:T(128)} %get-tuple-element.71, f32[128,255]{1,0:T(8,128)S(1)} %reshape.47), kind=kOutput, calls=%fused_computation.2 | convolution fusion | flops 808976384 | bytes 3245056 | tf_op jit(solution)/shard_map/while/body/eval_jaxpr/cond/branch_1_fun/dot_general | solution.py:37
  253.5 3.1 select_add_fusion.2
  260.0 5.0 %conditional.3 = (f32[128,4096]{1,0:T(8,128)S(1)}) conditional(s32[]{:T(128)} %bitcast.38, () %tuple.46, (s32[]{:T(128)}, s32[]{:T(128)}, f32[2176]{0:T(1024)S(1)}, bf16[16,128,4096]{2,1,0:T(8,128)(2,1)}, s32[]{:T(128)}, /*index=5*/f32[4096]{0:T(1024)S(1)}) %tuple.47), branch_computations={%region_2.2_spmd, %region_3.3_spmd} | conditional | flops 808980864 | bytes 4206158 | solution.py:83
  261.4 3.6 %fusion.1 = f32[128,4096]{1,0:T(8,128)S(1)} fusion(f32[128]{0:T(128)S(1)} %iota_add_fusion, f32[4096]{0:T(1024)S(1)} %neg.4, f32[4096]{0:T(1024)S(1)} %get-tuple-element.72, bf16[16,128,4096]{2,1,0:T(8,128)(2,1)} %get-tuple-element.70, s32[]{:T(128)} %get-tuple-element.71, f32[128,255]{1,0:T(8,128)S(1)} %reshape.47), kind=kOutput, calls=%fused_computation.2 | convolution fusion | flops 808976384 | bytes 3245056 | tf_op jit(solution)/shard_map/while/body/eval_jaxpr/cond/branch_1_fun/dot_general | solution.py:37
  265.0 3.1 select_add_fusion.2
  271.5 5.0 %conditional.3 = (f32[128,4096]{1,0:T(8,128)S(1)}) conditional(s32[]{:T(128)} %bitcast.38, () %tuple.46, (s32[]{:T(128)}, s32[]{:T(128)}, f32[2176]{0:T(1024)S(1)}, bf16[16,128,4096]{2,1,0:T(8,128)(2,1)}, s32[]{:T(128)}, /*index=5*/f32[4096]{0:T(1024)S(1)}) %tuple.47), branch_computations={%region_2.2_spmd, %region_3.3_spmd} | conditional | flops 808980864 | bytes 4206158 | solution.py:83
  272.9 3.6 %fusion.1 = f32[128,4096]{1,0:T(8,128)S(1)} fusion(f32[128]{0:T(128)S(1)} %iota_add_fusion, f32[4096]{0:T(1024)S(1)} %neg.4, f32[4096]{0:T(1024)S(1)} %get-tuple-element.72, bf16[16,128,4096]{2,1,0:T(8,128)(2,1)} %get-tuple-element.70, s32[]{:T(128)} %get-tuple-element.71, f32[128,255]{1,0:T(8,128)S(1)} %reshape.47), kind=kOutput, calls=%fused_computation.2 | convolution fusion | flops 808976384 | bytes 3245056 | tf_op jit(solution)/shard_map/while/body/eval_jaxpr/cond/branch_1_fun/dot_general | solution.py:37
  276.5 3.1 select_add_fusion.2
  283.1 5.0 %conditional.3 = (f32[128,4096]{1,0:T(8,128)S(1)}) conditional(s32[]{:T(128)} %bitcast.38, () %tuple.46, (s32[]{:T(128)}, s32[]{:T(128)}, f32[2176]{0:T(1024)S(1)}, bf16[16,128,4096]{2,1,0:T(8,128)(2,1)}, s32[]{:T(128)}, /*index=5*/f32[4096]{0:T(1024)S(1)}) %tuple.47), branch_computations={%region_2.2_spmd, %region_3.3_spmd} | conditional | flops 808980864 | bytes 4206158 | solution.py:83
  284.5 3.6 %fusion.1 = f32[128,4096]{1,0:T(8,128)S(1)} fusion(f32[128]{0:T(128)S(1)} %iota_add_fusion, f32[4096]{0:T(1024)S(1)} %neg.4, f32[4096]{0:T(1024)S(1)} %get-tuple-element.72, bf16[16,128,4096]{2,1,0:T(8,128)(2,1)} %get-tuple-element.70, s32[]{:T(128)} %get-tuple-element.71, f32[128,255]{1,0:T(8,128)S(1)} %reshape.47), kind=kOutput, calls=%fused_computation.2 | convolution fusion | flops 808976384 | bytes 3245056 | tf_op jit(solution)/shard_map/while/body/eval_jaxpr/cond/branch_1_fun/dot_general | solution.py:37
  288.1 3.1 select_add_fusion.2
  294.6 5.0 %conditional.3 = (f32[128,4096]{1,0:T(8,128)S(1)}) conditional(s32[]{:T(128)} %bitcast.38, () %tuple.46, (s32[]{:T(128)}, s32[]{:T(128)}, f32[2176]{0:T(1024)S(1)}, bf16[16,128,4096]{2,1,0:T(8,128)(2,1)}, s32[]{:T(128)}, /*index=5*/f32[4096]{0:T(1024)S(1)}) %tuple.47), branch_computations={%region_2.2_spmd, %region_3.3_spmd} | conditional | flops 808980864 | bytes 4206158 | solution.py:83
  296.0 3.6 %fusion.1 = f32[128,4096]{1,0:T(8,128)S(1)} fusion(f32[128]{0:T(128)S(1)} %iota_add_fusion, f32[4096]{0:T(1024)S(1)} %neg.4, f32[4096]{0:T(1024)S(1)} %get-tuple-element.72, bf16[16,128,4096]{2,1,0:T(8,128)(2,1)} %get-tuple-element.70, s32[]{:T(128)} %get-tuple-element.71, f32[128,255]{1,0:T(8,128)S(1)} %reshape.47), kind=kOutput, calls=%fused_computation.2 | convolution fusion | flops 808976384 | bytes 3245056 | tf_op jit(solution)/shard_map/while/body/eval_jaxpr/cond/branch_1_fun/dot_general | solution.py:37
  299.6 3.1 select_add_fusion.2
  302.7 5.6 %fusion.18 = bf16[128,4096]{1,0:T(8,128)(2,1)} fusion(f32[130,4096]{1,0:T(8,128)} %maximum_convert_fusion, f32[128,4096]{1,0:T(8,128)} %get-tuple-element.83, bf16[128,4096]{1,0:T(8,128)(2,1)S(1)} %copy-done, f32[4096]{0:T(1024)S(1)} %copy-done.4, f32[4096]{0:T(1024)S(1)} %bitcast.41, f32[4096]{0:T(1024)S(1)} %bitcast.42, f32[4096]{0:T(1024)S(1)} %bitcast.40), kind=kLoop, calls=%fused_computation.30 | loop fusion | flops 5242880 | bytes 10551296 | tf_op jit(solution)/shard_map/convert_element_type | solution.py:88
  (182 shorter events, 31.0 us)
Async XLA Ops:
  6.5 6.8 %copy-start.1 = (bf16[128,4096]{1,0:T(8,128)(2,1)S(1)}, bf16[128,4096]{1,0:T(8,128)(2,1)}, u32[]{:S(2)}) copy-start(bf16[128,4096]{1,0:T(8,128)(2,1)} %param.14) | copy-start | bytes 3145732
  6.5 137.1 %all-gather.2.cloned.1.call-start = ((), (), s32[]{:S(2)}) async-start(), calls=%async_computation | async-start | bytes 17825792 | tf_op jit(solution)/shard_map/all_gather | solution.py:70
  8.5 3.3 %collective-permute-start = (bf16[3,2,4096]{2,1,0:T(2,128)(2,1)S(1)}, bf16[3,2,4096]{2,1,0:T(2,128)(2,1)S(1)}, u32[]{:S(2)}, u32[]{:S(2)}) collective-permute-start(bf16[3,2,4096]{2,1,0:T(2,128)(2,1)S(1)} %pad_maximum_fusion.1), channel_id=1, source_target_pairs={{0,1},{1,2},{2,3},{3,4},{4,5},{5,6},{6,7},{7,8},{8,9},{9,10},{10,1... | collective-permute-start | bytes 147464 | tf_op jit(solution)/shard_map/ppermute | solution.py:10
  13.7 2.4 copy-start.5
  13.7 2.8 copy-start.6
  13.7 2.9 copy-start.2
  16.0 127.6 %copy-start.3 = (f32[4096]{0:T(1024)S(1)}, f32[4096]{0:T(1024)}, u32[]{:S(2)}) copy-start(f32[4096]{0:T(1024)} %param.16) | copy-start | bytes 49156
  143.6 159.1 %copy-start = (bf16[128,4096]{1,0:T(8,128)(2,1)S(1)}, bf16[128,4096]{1,0:T(8,128)(2,1)}, u32[]{:S(2)}) copy-start(bf16[128,4096]{1,0:T(8,128)(2,1)} %fusion.12) | copy-start | bytes 3145732
  143.6 159.1 %copy-start.4 = (f32[4096]{0:T(1024)S(1)}, f32[4096]{0:T(1024)}, u32[]{:S(2)}) copy-start(f32[4096]{0:T(1024)} %param.18) | copy-start | bytes 49156
Sparse Core Ops, SparseCore 0:
  16.1 127.4 all-gather.1
where the time goes:
time: 320 us; the launch traced here: 315 us
  waiting for transfers between devices  126 us (39%)
  other arithmetic  60.7 us (19%)
  loops' own time  43.3 us (14%)
  matrix products  39.5 us (12%)
  local copies, waits for them, and re-layouts  30.8 us (10%)
  between operations  13.5 us (4%)
    all_gather x1, waiting for transfers between devices, on_device(): lax.all_gather(gated, 'ctx', axis=0, tiled=True)  125 us
    add x16, other arithmetic, add_span(): carried + lax.cond(live_from[offset], compute_block, zero_block)  48.2 us
    dot_general x11, matrix products, block_term(): jnp.dot(toeplitz, scaled, precision=lax.Precision.HIGHEST, preferred_elem...  39.5 us
    another operation x1, loops' own time, on_device(): lax.scan(add_span, running, (jnp.arange(pieces.shape[0], dtype=jnp.int32)...  36.4 us
    dynamic_slice x16, local copies, waits for them, and re-layouts, add_span(): live_from[offset]  9.68 us
    dynamic_slice x16, local copies, waits for them, and re-layouts, on_device(): lax.scan(add_span, running, (jnp.arange(pieces.shape[0], dtype=jnp.int32)...  8.79 us
    another operation x16, loops' own time, add_span(): lax.cond(live_from[offset], compute_block, zero_block)  6.86 us
  transfers between devices with their start and end apart: 2, of which 2 were waited for; matrix products, arithmetic and copies ran while one was open for 1% of the time, Pallas kernels for 0%

commit v1 on v0

v1 whole, which is shorter than its diff:
```python
import functools

import jax
import jax.numpy as jnp
from jax import lax
from jax.experimental import pallas as pl
from jax.experimental.pallas import tpu as pltpu
from jax.sharding import PartitionSpec as P

MESH = pl.DeviceIdType.MESH


def kernel(
    n, rows, cw,
    q_ref, k_ref, v_ref, taps_ref, decay_ref, lag_ref, skip_ref, keep_ref,
    out_ref,
    rim_out, rim_in, gated, qfeat, spans, scaled, masked, toep, result, landed,
    rim_sem, send1, recv1, send2, recv2,
):
    me = lax.axis_index("ctx")
    wide = 2 * rows
    half = n // 2

    barrier = pltpu.get_barrier_semaphore()

    def greet(k, c):
        p = lax.rem(me + k, n)
        pl.semaphore_signal(barrier, inc=1, device_id={"ctx": p}, device_id_type=MESH)
        return c

    lax.fori_loop(1, n, greet, 0)

    for index, ref in enumerate((q_ref, k_ref, v_ref)):
        tail = ref[rows - 16 :, :].astype(jnp.float32)
        rim_out[2 * index : 2 * index + 2, :] = tail[14:16]
    rim_out[6:8, :] = jnp.zeros((2, rim_out.shape[1]), jnp.float32)

    pl.semaphore_wait(barrier, n - 1)

    def rim_copy(to):
        return pltpu.make_async_remote_copy(
            src_ref=rim_out, dst_ref=rim_in, send_sem=rim_sem.at[0], recv_sem=rim_sem.at[1],
            device_id={"ctx": to}, device_id_type=MESH,
        )

    @pl.when(me < n - 1)
    def _():
        rim_copy(me + 1).start()

    @pl.when(me == 0)
    def _():
        rim_in[...] = jnp.zeros_like(rim_in)

    @pl.when(me > 0)
    def _():
        rim_copy(me - 1).wait_recv()

    row = lax.broadcasted_iota(jnp.int32, (rows, cw), 0)

    def feature(ref, index, cols):
        x = ref[:, cols].astype(jnp.float32)
        one = rim_in[2 * index + 1 : 2 * index + 2, cols]
        two = rim_in[2 * index : 2 * index + 1, cols]
        x1 = jnp.where(row == 0, one, pltpu.roll(x, 1, 0))
        x2 = jnp.where(row == 0, two, jnp.where(row == 1, one, pltpu.roll(x, 2, 0)))
        return (
            taps_ref[index, 0:1, cols] * x
            + taps_ref[index, 1:2, cols] * x1
            + taps_ref[index, 2:3, cols] * x2
        )

    def columns(p):
        return pl.ds(pl.multiple_of(p * cw, cw), cw)

    def forward(p, sender):
        return pltpu.make_async_remote_copy(
            src_ref=gated.at[p], dst_ref=spans.at[sender],
            send_sem=send1.at[p], recv_sem=recv1.at[sender],
            device_id={"ctx": p}, device_id_type=MESH,
        )

    def backward(p, sender):
        return pltpu.make_async_remote_copy(
            src_ref=result.at[p], dst_ref=landed.at[sender],
            send_sem=send2.at[p], recv_sem=recv2.at[sender],
            device_id={"ctx": p}, device_id_type=MESH,
        )

    def gate(k, c):
        p = lax.rem(me + half + k, n)
        cols = columns(p)
        value = (feature(k_ref, 1, cols) * feature(v_ref, 2, cols)).astype(jnp.bfloat16)
        gated[p] = value

        @pl.when(p != me)
        def _():
            forward(p, me).start()

        @pl.when(p == me)
        def _():
            spans[me] = value

        return c

    lax.fori_loop(0, n, gate, 0)

    def build(d, c):
        upper = lag_ref[:, pl.ds(pl.multiple_of(d * wide, wide), wide)]
        below = jnp.maximum(d - 1, 0)
        lower = lag_ref[:, pl.ds(pl.multiple_of(below * wide, wide), wide)]
        lower = jnp.where(d > 0, lower, 0.0)
        window = jnp.broadcast_to(jnp.concatenate([upper, lower], axis=1), (wide, 2 * wide))
        turned = pltpu.roll(window, 0, 1, stride=1, stride_axis=0)[:, :wide]
        toep[d] = turned.T.astype(jnp.bfloat16)
        return c

    lax.fori_loop(0, half, build, 0)

    def query(p, c):
        qfeat[p] = feature(q_ref, 0, columns(p))
        return c

    lax.fori_loop(0, n, query, 0)

    rate = decay_ref[:, columns(me)]
    place = lax.broadcasted_iota(jnp.int32, (wide, cw), 0).astype(jnp.float32)
    grow = jnp.exp(rate * place)
    fade = jnp.exp(-rate * place)
    step_fade = jnp.exp(-rate * wide)

    def keep_of(j):
        return keep_ref[pl.ds(j, 1), 0:1]

    def target(i, c):
        for part in range(2):
            source = 2 * i + part

            @pl.when(source != me)
            def _():
                forward(me, source).wait_recv()

        first = spans[2 * i].astype(jnp.float32) * grow[:rows]
        second = spans[2 * i + 1].astype(jnp.float32) * grow[rows:]
        keep_first = keep_of(2 * i)
        keep_second = keep_of(2 * i + 1)
        scaled[i, 0:rows, :] = first.astype(jnp.bfloat16)
        masked[i, 0:rows, :] = (first * keep_second).astype(jnp.bfloat16)
        masked[i, rows:wide, :] = second.astype(jnp.bfloat16)

        def source_step(j, acc):
            both = keep_of(2 * j) * keep_of(2 * j + 1)
            return acc * (step_fade * both) + jnp.dot(
                toep[i - j], masked[j], preferred_element_type=jnp.float32
            )

        acc = lax.fori_loop(0, i, source_step, jnp.zeros((wide, cw), jnp.float32))
        top = acc[:rows] * (step_fade * keep_first) + jnp.dot(
            toep[0, 0:rows, 0:rows], scaled[i, 0:rows, :], preferred_element_type=jnp.float32
        )
        bottom = acc[rows:] * (step_fade * keep_first * keep_second) + jnp.dot(
            toep[0, rows:wide, :], masked[i], preferred_element_type=jnp.float32
        )
        for part, value in enumerate((top * fade[:rows], bottom * fade[rows:])):
            reader = 2 * i + part
            value = value.astype(jnp.bfloat16)
            result[reader] = value

            @pl.when(reader != me)
            def _():
                backward(reader, me).start()

            @pl.when(reader == me)
            def _():
                landed[me] = value

        return c

    lax.fori_loop(0, half, target, 0)

    def finish(k, c):
        p = lax.rem(me + k, n)

        @pl.when(p != me)
        def _():
            backward(me, p).wait_recv()

        cols = columns(p)
        direct = skip_ref[:, cols] * gated[p].astype(jnp.float32)
        out_ref[:, cols] = (qfeat[p] * (landed[p].astype(jnp.float32) + direct)).astype(
            jnp.bfloat16
        )
        return c

    lax.fori_loop(0, n, finish, 0)

    def drain(k, c):
        p = lax.rem(me + k, n)
        forward(p, me).wait_send()
        backward(p, me).wait_send()
        return c

    lax.fori_loop(1, n, drain, 0)

    @pl.when(me < n - 1)
    def _():
        rim_copy(me + 1).wait_send()


def on_device(
    query_rows, key_rows, value_rows, conv_taps, decay_rate, lag_profile, skip_gain, pair_lists
):
    rows, channels = query_rows.shape
    n = lax.axis_size("ctx")
    cw = channels // n
    half = n // 2
    wide = 2 * rows
    sources, targets = pair_lists[:, :, 0], pair_lists[:, :, 1]
    border = 1 + jnp.max(jnp.where(sources == 0, targets, -1))
    keep = (lax.broadcasted_iota(jnp.int32, (n, 128), 0) != border).astype(jnp.float32)
    vmem = pl.BlockSpec(memory_space=pltpu.VMEM)
    return pl.pallas_call(
        functools.partial(kernel, n, rows, cw),
        out_shape=jax.ShapeDtypeStruct((rows, channels), jnp.bfloat16),
        in_specs=[vmem] * 8,
        out_specs=vmem,
        scratch_shapes=[
            pltpu.VMEM((8, channels), jnp.float32),
            pltpu.VMEM((8, channels), jnp.float32),
            pltpu.VMEM((n, rows, cw), jnp.bfloat16),
            pltpu.VMEM((n, rows, cw), jnp.float32),
            pltpu.VMEM((n, rows, cw), jnp.bfloat16),
            pltpu.VMEM((half, wide, cw), jnp.bfloat16),
            pltpu.VMEM((half, wide, cw), jnp.bfloat16),
            pltpu.VMEM((half, wide, wide), jnp.bfloat16),
            pltpu.VMEM((n, rows, cw), jnp.bfloat16),
            pltpu.VMEM((n, rows, cw), jnp.bfloat16),
            pltpu.SemaphoreType.DMA((2,)),
            pltpu.SemaphoreType.DMA((n,)),
            pltpu.SemaphoreType.DMA((n,)),
            pltpu.SemaphoreType.DMA((n,)),
            pltpu.SemaphoreType.DMA((n,)),
        ],
        compiler_params=pltpu.CompilerParams(
            collective_id=0, has_side_effects=True, vmem_limit_bytes=48 * 1024 * 1024
        ),
    )(
        query_rows, key_rows, value_rows, conv_taps, decay_rate.reshape(1, -1),
        lag_profile.reshape(1, -1), skip_gain.reshape(1, -1), keep,
    )


def solution(mesh):
    rows = P(("group", "ctx"), None)
    return jax.shard_map(
        on_device,
        mesh=mesh,
        in_specs=(rows, rows, rows, P(), P(), P(), P(), P("group", None, None)),
        out_specs=rows,
        check_vma=False,
    )
```

time: 320 us -> 70.5 us (0.22); the launches traced: 315 us -> 70.1 us
  waiting for transfers between devices: 126 us -> 0 us
  Pallas kernels: 0 us -> 61 us
  other arithmetic: 60.7 us -> 1.43 us
  loops' own time: 43.3 us -> 0 us
  matrix products: 39.5 us -> 0 us
  local copies, waits for them, and re-layouts: 30.8 us -> 6.97 us
  between operations: 13.5 us -> 0.68 us
    all_gather x1 -> x0, waiting for transfers between devices: 125 us -> none  [on_device(): lax.all_gather(gated, 'ctx', axis=0, tiled=True)]
    pallas_call x0 -> x1, Pallas kernels: none -> 61 us  [on_device(): pl.pallas_call(functools.partial(kernel, n, rows, cw), out_shape=jax.Shap...]
    add x27 -> x0, other arithmetic: 48.3 us -> none  [the longest x16 48.2 us: add_span(): carried + lax.cond(live_from[offset], compute_block, zero_block)]
    another operation x17 -> x0, loops' own time: 43.3 us -> none  [the longest x1 36.4 us: on_device(): lax.scan(add_span, running, (jnp.arange(pieces.shape[0], dtype=jnp.int32)...]
    dot_general x11 -> x0, matrix products: 39.5 us -> none  [block_term(): jnp.dot(toeplitz, scaled, precision=lax.Precision.HIGHEST, preferred_elem...]
    dynamic_slice x43 -> x0, local copies, waits for them, and re-layouts: 19.3 us -> none  [the longest x16 9.68 us: add_span(): live_from[offset]]
    convert_element_type x5 -> x1, other arithmetic: 11.3 us -> 0.01 us  [on_device(): (lax.broadcasted_iota(jnp.int32, (n, 128), 0) != border).astype(jnp.float32)]
    unnamed x14 -> x15, local copies, waits for them, and re-layouts: 0.03 us -> 6.9 us
  transfers between devices with their start and end apart: 2 -> 0, of which waited for: 2 -> 0; matrix products, arithmetic and copies ran while one was open for 1% -> 0% of each run, Pallas kernels for 0% -> 0%
where the time goes in v1:
time: 70.5 us; the launch traced here: 70.1 us
  Pallas kernels  61 us (87%)
  local copies, waits for them, and re-layouts  6.97 us (10%)
  other arithmetic  1.43 us (2%)
    pallas_call x1, Pallas kernels, on_device(): pl.pallas_call(functools.partial(kernel, n, rows, cw), out_shape=jax.Shap...  61 us
    unnamed x15, local copies, waits for them, and re-layouts  6.9 us
    reduce_max x1, other arithmetic, on_device(): border = 1 + jnp.max(jnp.where(sources == 0, targets, -1))  1.42 us

profile of v1, /device:TPU:29, one launch (start us, length us, event | category | flops | bytes accessed | tf_op | source)
XLA Modules:
  0.0 70.1 jit_solution(9086407904065779013)
XLA Ops:
  0.0 0.0 copy-start.4
  0.0 1.4 %fusion = s32[]{:T(128)} fusion(s32[16,9,2]{0,2,1:T(2,128)} %param.15), kind=kLoop, calls=%fused_computation.1 | loop fusion | flops 431 | bytes 1156 | tf_op jit(solution)/shard_map/reduce_max | solution.py:218
  2.1 0.0 copy-start.6
  2.1 0.1 iota.7.keep_ref
  2.2 0.0 copy-done.4
  2.2 0.6 copy-done.6
  2.8 0.0 copy-start
  2.8 1.2 %copy-done = bf16[128,4096]{1,0:T(8,128)(2,1)S(1)} copy-done((bf16[128,4096]{1,0:T(8,128)(2,1)S(1)}, bf16[128,4096]{1,0:T(8,128)(2,1)}, u32[]{:S(2)}) %copy-start) | copy-done | bytes 1048600
  4.0 0.0 copy-start.1
  4.0 1.2 %copy-done.1 = bf16[128,4096]{1,0:T(8,128)(2,1)S(1)} copy-done((bf16[128,4096]{1,0:T(8,128)(2,1)S(1)}, bf16[128,4096]{1,0:T(8,128)(2,1)}, u32[]{:S(2)}) %copy-start.1) | copy-done | bytes 1048600
  5.2 0.0 copy-start.2
  5.2 1.2 %copy-done.2 = bf16[128,4096]{1,0:T(8,128)(2,1)S(1)} copy-done((bf16[128,4096]{1,0:T(8,128)(2,1)S(1)}, bf16[128,4096]{1,0:T(8,128)(2,1)}, u32[]{:S(2)}) %copy-start.2) | copy-done | bytes 1048600
  6.5 0.0 copy-start.3
  6.5 0.9 %copy-done.3 = f32[3,3,4096]{2,1,0:T(4,128)S(1)} copy-done((f32[3,3,4096]{2,1,0:T(4,128)S(1)}, f32[3,3,4096]{2,1,0:T(4,128)}, u32[]{:S(2)}) %copy-start.3) | copy-done | bytes 147480
  7.4 0.0 copy-start.5
  7.4 0.7 %copy-done.5 = f32[4096]{0:T(1024)S(1)} copy-done((f32[4096]{0:T(1024)S(1)}, f32[4096]{0:T(1024)}, u32[]{:S(2)}) %copy-start.5) | copy-done | bytes 16408
  8.1 61.0 %shard_map.82 = bf16[128,4096]{1,0:T(8,128)(2,1)S(1)} custom-call(bf16[128,4096]{1,0:T(8,128)(2,1)S(1)} %copy-done, bf16[128,4096]{1,0:T(8,128)(2,1)S(1)} %copy-done.1, bf16[128,4096]{1,0:T(8,128)(2,1)S(1)} %copy-done.2, f32[3,3,4096]{2,1,0:T(4,128)S(1)} %copy-done.3, f32[1,4096]{1,0:T(1,128)S(1)} %bitcast.3, f32[1,2048]{1,0:T(1,128)S(1)} %bitcast.5, ...), custom_call_target="tpu_custom_call" | custom-call | tf_op jit(solution)/shard_map/pallas_call | solution.py:221
  69.2 1.0 %copy.10 = bf16[128,4096]{1,0:T(8,128)(2,1)} copy(bf16[128,4096]{1,0:T(8,128)(2,1)S(1)} %shard_map.82) | data formatting | bytes 2097152
  (1 shorter events, 0.0 us)
Async XLA Ops:
  0.0 2.2 %copy-start.4 = (f32[4096]{0:T(1024)S(1)}, f32[4096]{0:T(1024)}, u32[]{:S(2)}) copy-start(f32[4096]{0:T(1024)} %param.12) | copy-start | bytes 49156
  2.1 0.7 copy-start.6
  2.8 1.2 %copy-start = (bf16[128,4096]{1,0:T(8,128)(2,1)S(1)}, bf16[128,4096]{1,0:T(8,128)(2,1)}, u32[]{:S(2)}) copy-start(bf16[128,4096]{1,0:T(8,128)(2,1)} %q_ref.1) | copy-start | bytes 3145732
  4.0 1.2 %copy-start.1 = (bf16[128,4096]{1,0:T(8,128)(2,1)S(1)}, bf16[128,4096]{1,0:T(8,128)(2,1)}, u32[]{:S(2)}) copy-start(bf16[128,4096]{1,0:T(8,128)(2,1)} %k_ref.1) | copy-start | bytes 3145732
  5.2 1.2 %copy-start.2 = (bf16[128,4096]{1,0:T(8,128)(2,1)S(1)}, bf16[128,4096]{1,0:T(8,128)(2,1)}, u32[]{:S(2)}) copy-start(bf16[128,4096]{1,0:T(8,128)(2,1)} %v_ref.1) | copy-start | bytes 3145732
  6.5 0.9 %copy-start.3 = (f32[3,3,4096]{2,1,0:T(4,128)S(1)}, f32[3,3,4096]{2,1,0:T(4,128)}, u32[]{:S(2)}) copy-start(f32[3,3,4096]{2,1,0:T(4,128)} %taps_ref.1) | copy-start | bytes 442372
  7.4 0.7 %copy-start.5 = (f32[4096]{0:T(1024)S(1)}, f32[4096]{0:T(1024)}, u32[]{:S(2)}) copy-start(f32[4096]{0:T(1024)} %param.14) | copy-start | bytes 49156

commit v2 on v1

v2 whole, which is shorter than its diff:
```python
import functools

import jax
import jax.numpy as jnp
from jax import lax
from jax.experimental import pallas as pl
from jax.experimental.pallas import tpu as pltpu
from jax.sharding import PartitionSpec as P

MESH = pl.DeviceIdType.MESH
CHUNK = 256


def kernel(
    n, rows, chunks, width,
    q_hbm, k_hbm, v_hbm, taps_hbm, decay_ref, lag_ref, skip_ref, keep_ref,
    out_ref,
    q_ref, k_ref, v_ref, taps_ref, rim_out, rim_in, gated, qfeat, spans, scaled, masked, toep,
    outbox, inbox, start_acc, result, landed,
    load_sem, rim_sem, send1, recv1, send2, recv2, send_box, recv_box,
):
    me = lax.axis_index("ctx")
    wide = 2 * rows
    members = n // 2
    supers = n // 4
    boxed = n // 8
    part = me // members
    base = part * members
    mine = me - base

    loads = [
        pltpu.make_async_copy(src, dst, load_sem.at[index])
        for index, (src, dst) in enumerate(
            ((k_hbm, k_ref), (v_hbm, v_ref), (taps_hbm, taps_ref), (q_hbm, q_ref))
        )
    ]
    for load in loads:
        load.start()

    barrier = pltpu.get_barrier_semaphore()

    def greet(k, c):
        p = lax.rem(me + k, n)
        pl.semaphore_signal(barrier, inc=1, device_id={"ctx": p}, device_id_type=MESH)
        return c

    lax.fori_loop(1, n, greet, 0)
    for load in loads:
        load.wait()

    for index, ref in enumerate((q_ref, k_ref, v_ref)):
        tail = ref[rows - 16 :, :].astype(jnp.float32)
        rim_out[2 * index : 2 * index + 2, :] = tail[14:16]
    rim_out[6:8, :] = jnp.zeros((2, rim_out.shape[1]), jnp.float32)

    pl.semaphore_wait(barrier, n - 1)

    def rim_copy(to):
        return pltpu.make_async_remote_copy(
            src_ref=rim_out, dst_ref=rim_in, send_sem=rim_sem.at[0], recv_sem=rim_sem.at[1],
            device_id={"ctx": to}, device_id_type=MESH,
        )

    @pl.when(me < n - 1)
    def _():
        rim_copy(me + 1).start()

    @pl.when(me == 0)
    def _():
        rim_in[...] = jnp.zeros_like(rim_in)

    def build(d, c):
        upper = lag_ref[:, pl.ds(pl.multiple_of(d * wide, wide), wide)]
        below = jnp.maximum(d - 1, 0)
        lower = lag_ref[:, pl.ds(pl.multiple_of(below * wide, wide), wide)]
        lower = jnp.where(d > 0, lower, 0.0)
        window = jnp.broadcast_to(jnp.concatenate([upper, lower], axis=1), (wide, 2 * wide))
        turned = pltpu.roll(window, 0, 1, stride=1, stride_axis=0)[:, :wide]
        toep[d] = turned.T.astype(jnp.bfloat16)
        return c

    @pl.when(me > 0)
    def _():
        rim_copy(me - 1).wait_recv()

    row = lax.broadcasted_iota(jnp.int32, (rows, width), 0)

    def feature(ref, index, cols):
        x = ref[:, cols].astype(jnp.float32)
        one = rim_in[2 * index + 1 : 2 * index + 2, cols]
        two = rim_in[2 * index : 2 * index + 1, cols]
        x1 = jnp.where(row == 0, one, pltpu.roll(x, 1, 0))
        x2 = jnp.where(row == 0, two, jnp.where(row == 1, one, pltpu.roll(x, 2, 0)))
        return (
            taps_ref[index, 0:1, cols] * x
            + taps_ref[index, 1:2, cols] * x1
            + taps_ref[index, 2:3, cols] * x2
        )

    def columns(c, p):
        return pl.ds(pl.multiple_of((p * chunks + c) * width, width), width)

    def forward(c, p, sender):
        return pltpu.make_async_remote_copy(
            src_ref=gated.at[c, p], dst_ref=spans.at[c, sender],
            send_sem=send1.at[c, p], recv_sem=recv1.at[c, sender],
            device_id={"ctx": base + p}, device_id_type=MESH,
        )

    def backward(c, p, sender):
        return pltpu.make_async_remote_copy(
            src_ref=result.at[c, p], dst_ref=landed.at[c, sender],
            send_sem=send2.at[c, p], recv_sem=recv2.at[c, sender],
            device_id={"ctx": base + p}, device_id_type=MESH,
        )

    def box_copy(c, to):
        return pltpu.make_async_remote_copy(
            src_ref=outbox.at[c], dst_ref=inbox.at[c],
            send_sem=send_box.at[c], recv_sem=recv_box.at[c],
            device_id={"ctx": to}, device_id_type=MESH,
        )

    for c in range(chunks):

        def gate(k, carry, c=c):
            p = lax.rem(mine + members // 2 + k, members)
            cols = columns(c, p)
            value = (feature(k_ref, 1, cols) * feature(v_ref, 2, cols)).astype(jnp.bfloat16)
            gated[c, p] = value

            @pl.when(p != mine)
            def _():
                forward(c, p, mine).start()

            @pl.when(p == mine)
            def _():
                spans[c, mine] = value

            return carry

        lax.fori_loop(0, members, gate, 0)

    lax.fori_loop(0, n // 2, build, 0)

    place = lax.broadcasted_iota(jnp.int32, (wide, width), 0).astype(jnp.float32)

    def rate_of(c):
        return decay_ref[:, columns(c, mine)]

    def keep_of(j):
        return keep_ref[pl.ds(j, 1), 0:1]

    early = keep_ref[n : n + 1, 0:1] > 0.5

    def matmul(a, b):
        return jnp.dot(a, b, preferred_element_type=jnp.float32)

    def prepare(c):
        grow = jnp.exp(rate_of(c) * place)

        def scale(i, carry):
            for side in range(2):
                source = 2 * i + side

                @pl.when(source != mine)
                def _():
                    forward(c, mine, source).wait_recv()

            first = spans[c, 2 * i].astype(jnp.float32) * grow[:rows]
            second = (spans[c, 2 * i + 1].astype(jnp.float32) * grow[rows:]).astype(jnp.bfloat16)
            scaled[c, i] = first.astype(jnp.bfloat16)
            masked[c, i, 0:rows, :] = (first * keep_of(base + 2 * i + 1)).astype(jnp.bfloat16)
            masked[c, i, rows:wide, :] = second
            return carry

        lax.fori_loop(0, supers, scale, 0)

    def post(c):
        step_fade = jnp.exp(-rate_of(c) * wide)
        for m in range(boxed):
            acc = matmul(toep[supers + m], masked[c, 0])
            for j in range(1, supers):
                acc = acc * step_fade + matmul(toep[supers + m - j], masked[c, j])
            source = masked[c, supers - boxed + m].astype(jnp.float32)
            outbox[c, m] = jnp.where(early, source, acc).astype(jnp.bfloat16)
        box_copy(c, me + members).start()

    def local(c):
        rate = rate_of(c)
        fade = jnp.exp(-rate * place)
        step_fade = jnp.exp(-rate * wide)

        def target(i, carry):
            @pl.when(part == 0)
            def _():
                start_acc[...] = jnp.zeros_like(start_acc)

            @pl.when(part == 1)
            def _():
                acc = matmul(toep[i + boxed], inbox[c, 0])
                for m in range(1, boxed):
                    span = 2 * (supers - boxed + m)
                    both = keep_of(span) * keep_of(span + 1)
                    acc = acc * (step_fade * both) + matmul(toep[i + boxed - m], inbox[c, m])
                partial = inbox[c, jnp.minimum(i, boxed - 1)].astype(jnp.float32)
                partial = jnp.where(i < boxed, partial, 0.0)
                start_acc[...] = jnp.where(early, acc, partial)

            def source_step(j, acc):
                span = base + 2 * j
                both = keep_of(span) * keep_of(span + 1)
                return acc * (step_fade * both) + matmul(toep[i - j], masked[c, j])

            acc = lax.fori_loop(0, i, source_step, start_acc[...])
            keep_first = keep_of(base + 2 * i)
            keep_second = keep_of(base + 2 * i + 1)
            top = acc[:rows] * (step_fade * keep_first) + matmul(
                toep[0, 0:rows, 0:rows], scaled[c, i]
            )
            bottom = acc[rows:] * (step_fade * keep_first * keep_second) + matmul(
                toep[0, rows:wide, :], masked[c, i]
            )
            for side, value in enumerate((top * fade[:rows], bottom * fade[rows:])):
                reader = 2 * i + side
                value = value.astype(jnp.bfloat16)
                result[c, reader] = value

                @pl.when(reader != mine)
                def _():
                    backward(c, reader, mine).start()

                @pl.when(reader == mine)
                def _():
                    landed[c, mine] = value

            return carry

        lax.fori_loop(0, supers, target, 0)

    for c in range(chunks):
        prepare(c)

        @pl.when(part == 0)
        def _():
            post(c)

    def query(p, carry):
        for c in range(chunks):
            qfeat[c, p] = feature(q_ref, 0, columns(c, p))
        return carry

    lax.fori_loop(0, members, query, 0)

    for c in range(chunks):

        @pl.when(part == 1)
        def _():
            box_copy(c, me - members).wait_recv()

        local(c)

    for c in range(chunks):

        def finish(k, carry, c=c):
            p = lax.rem(mine + k, members)

            @pl.when(p != mine)
            def _():
                backward(c, mine, p).wait_recv()

            cols = columns(c, p)
            direct = skip_ref[:, cols] * gated[c, p].astype(jnp.float32)
            out_ref[:, cols] = (
                qfeat[c, p] * (landed[c, p].astype(jnp.float32) + direct)
            ).astype(jnp.bfloat16)
            return carry

        lax.fori_loop(0, members, finish, 0)

    def drain(k, carry):
        p = lax.rem(mine + k, members)
        for c in range(chunks):
            forward(c, p, mine).wait_send()
            backward(c, p, mine).wait_send()
        return carry

    lax.fori_loop(1, members, drain, 0)

    @pl.when(part == 0)
    def _():
        for c in range(chunks):
            box_copy(c, me + members).wait_send()

    @pl.when(me < n - 1)
    def _():
        rim_copy(me + 1).wait_send()


def on_device(
    query_rows, key_rows, value_rows, conv_taps, decay_rate, lag_profile, skip_gain, pair_lists
):
    rows, channels = query_rows.shape
    n = lax.axis_size("ctx")
    members, supers, boxed, wide = n // 2, n // 4, n // 8, 2 * rows
    share = channels // members
    width = min(CHUNK, max(128, share // 2))
    chunks = share // width
    sources, targets = pair_lists[:, :, 0], pair_lists[:, :, 1]
    border = 1 + jnp.max(jnp.where(sources == 0, targets, -1))
    index = lax.broadcasted_iota(jnp.int32, (n + 8, 128), 0)
    keep = jnp.where(index == n, border <= members, index != border).astype(jnp.float32)
    vmem = pl.BlockSpec(memory_space=pltpu.VMEM)
    hbm = pl.BlockSpec(memory_space=pltpu.HBM)
    bf16, f32 = jnp.bfloat16, jnp.float32
    piece = (chunks, members, rows, width)
    dma = pltpu.SemaphoreType.DMA
    return pl.pallas_call(
        functools.partial(kernel, n, rows, chunks, width),
        out_shape=jax.ShapeDtypeStruct((rows, channels), bf16),
        in_specs=[hbm] * 4 + [vmem] * 4,
        out_specs=vmem,
        scratch_shapes=[
            pltpu.VMEM((rows, channels), bf16),
            pltpu.VMEM((rows, channels), bf16),
            pltpu.VMEM((rows, channels), bf16),
            pltpu.VMEM(conv_taps.shape, f32),
            pltpu.VMEM((8, channels), f32),
            pltpu.VMEM((8, channels), f32),
            pltpu.VMEM(piece, bf16),
            pltpu.VMEM(piece, f32),
            pltpu.VMEM(piece, bf16),
            pltpu.VMEM((chunks, supers, rows, width), bf16),
            pltpu.VMEM((chunks, supers, wide, width), bf16),
            pltpu.VMEM((n // 2, wide, wide), bf16),
            pltpu.VMEM((chunks, boxed, wide, width), bf16),
            pltpu.VMEM((chunks, boxed, wide, width), bf16),
            pltpu.VMEM((wide, width), f32),
            pltpu.VMEM(piece, bf16),
            pltpu.VMEM(piece, bf16),
            dma((4,)),
            dma((2,)),
            dma((chunks, members)),
            dma((chunks, members)),
            dma((chunks, members)),
            dma((chunks, members)),
            dma((chunks,)),
            dma((chunks,)),
        ],
        compiler_params=pltpu.CompilerParams(
            collective_id=0, has_side_effects=True, vmem_limit_bytes=48 * 1024 * 1024
        ),
    )(
        query_rows, key_rows, value_rows, conv_taps, decay_rate.reshape(1, -1),
        lag_profile.reshape(1, -1), skip_gain.reshape(1, -1), keep,
    )


def solution(mesh):
    rows = P(("group", "ctx"), None)
    return jax.shard_map(
        on_device,
        mesh=mesh,
        in_specs=(rows, rows, rows, P(), P(), P(), P(), P("group", None, None)),
        out_specs=rows,
        check_vma=False,
    )
```

time: 70.5 us -> 60.2 us (0.85)
  Pallas kernels: 61 us -> 51.4 us
    pallas_call x1, Pallas kernels: 61 us -> 51.4 us  [on_device(): pl.pallas_call(functools.partial(kernel, n, rows, chunks, width), out_sha...]
where the time goes in v2:
time: 60.2 us; the launch traced here: 59.9 us
  Pallas kernels  51.4 us (85%)
  local copies, waits for them, and re-layouts  6.35 us (11%)
  other arithmetic  1.43 us (2%)
  between operations  0.68 us (1%)
    pallas_call x1, Pallas kernels, on_device(): pl.pallas_call(functools.partial(kernel, n, rows, chunks, width), out_sha...  51.4 us
    unnamed x15, local copies, waits for them, and re-layouts  6.28 us
    reduce_max x1, other arithmetic, on_device(): border = 1 + jnp.max(jnp.where(sources == 0, targets, -1))  1.42 us

profile of v2, /device:TPU:29, one launch (start us, length us, event | category | flops | bytes accessed | tf_op | source)
XLA Modules:
  0.0 59.9 jit_solution(18128449439801066666)
XLA Ops:
  0.0 0.0 copy-start.5
  0.0 0.0 copy-start.4
  0.0 1.4 %fusion = s32[]{:T(128)} fusion(s32[16,9,2]{0,2,1:T(2,128)} %param.15), kind=kLoop, calls=%fused_computation.1 | loop fusion | flops 431 | bytes 1156 | tf_op jit(solution)/shard_map/reduce_max | solution.py:310
  2.1 0.1 iota.10.keep_ref
  2.2 0.0 copy-done.5
  2.2 0.0 copy-done.4
  2.2 0.0 copy-start
  2.2 1.2 %copy-done = bf16[128,4096]{1,0:T(8,128)(2,1)S(1)} copy-done((bf16[128,4096]{1,0:T(8,128)(2,1)S(1)}, bf16[128,4096]{1,0:T(8,128)(2,1)}, u32[]{:S(2)}) %copy-start) | copy-done | bytes 1048600
  3.4 0.0 copy-start.1
  3.4 1.2 %copy-done.1 = bf16[128,4096]{1,0:T(8,128)(2,1)S(1)} copy-done((bf16[128,4096]{1,0:T(8,128)(2,1)S(1)}, bf16[128,4096]{1,0:T(8,128)(2,1)}, u32[]{:S(2)}) %copy-start.1) | copy-done | bytes 1048600
  4.6 0.0 copy-start.2
  4.6 1.2 %copy-done.2 = bf16[128,4096]{1,0:T(8,128)(2,1)S(1)} copy-done((bf16[128,4096]{1,0:T(8,128)(2,1)S(1)}, bf16[128,4096]{1,0:T(8,128)(2,1)}, u32[]{:S(2)}) %copy-start.2) | copy-done | bytes 1048600
  5.8 0.0 copy-start.3
  5.9 0.9 %copy-done.3 = f32[3,3,4096]{2,1,0:T(4,128)S(1)} copy-done((f32[3,3,4096]{2,1,0:T(4,128)S(1)}, f32[3,3,4096]{2,1,0:T(4,128)}, u32[]{:S(2)}) %copy-start.3) | copy-done | bytes 147480
  6.8 0.0 copy-start.6
  6.8 0.7 %copy-done.6 = f32[2048]{0:T(1024)S(1)} copy-done((f32[2048]{0:T(1024)S(1)}, f32[2048]{0:T(1024)}, u32[]{:S(2)}) %copy-start.6) | copy-done | bytes 8216
  7.5 51.4 %shard_map.82 = bf16[128,4096]{1,0:T(8,128)(2,1)S(1)} custom-call(bf16[128,4096]{1,0:T(8,128)(2,1)S(1)} %copy-done, bf16[128,4096]{1,0:T(8,128)(2,1)S(1)} %copy-done.1, bf16[128,4096]{1,0:T(8,128)(2,1)S(1)} %copy-done.2, f32[3,3,4096]{2,1,0:T(4,128)S(1)} %copy-done.3, f32[1,4096]{1,0:T(1,128)S(1)} %bitcast.3, f32[1,2048]{1,0:T(1,128)S(1)} %bitcast.5, ...), custom_call_target="tpu_custom_call" | custom-call | tf_op jit(solution)/shard_map/pallas_call | solution.py:318
  58.9 1.0 %copy.10 = bf16[128,4096]{1,0:T(8,128)(2,1)} copy(bf16[128,4096]{1,0:T(8,128)(2,1)S(1)} %shard_map.82) | data formatting | bytes 2097152
  (1 shorter events, 0.0 us)
Async XLA Ops:
  0.0 2.2 %copy-start.5 = (f32[4096]{0:T(1024)S(1)}, f32[4096]{0:T(1024)}, u32[]{:S(2)}) copy-start(f32[4096]{0:T(1024)} %param.14) | copy-start | bytes 49156
  0.0 2.2 %copy-start.4 = (f32[4096]{0:T(1024)S(1)}, f32[4096]{0:T(1024)}, u32[]{:S(2)}) copy-start(f32[4096]{0:T(1024)} %param.12) | copy-start | bytes 49156
  2.2 1.2 %copy-start = (bf16[128,4096]{1,0:T(8,128)(2,1)S(1)}, bf16[128,4096]{1,0:T(8,128)(2,1)}, u32[]{:S(2)}) copy-start(bf16[128,4096]{1,0:T(8,128)(2,1)} %q_hbm.1) | copy-start | bytes 3145732
  3.4 1.2 %copy-start.1 = (bf16[128,4096]{1,0:T(8,128)(2,1)S(1)}, bf16[128,4096]{1,0:T(8,128)(2,1)}, u32[]{:S(2)}) copy-start(bf16[128,4096]{1,0:T(8,128)(2,1)} %k_hbm.1) | copy-start | bytes 3145732
  4.6 1.2 %copy-start.2 = (bf16[128,4096]{1,0:T(8,128)(2,1)S(1)}, bf16[128,4096]{1,0:T(8,128)(2,1)}, u32[]{:S(2)}) copy-start(bf16[128,4096]{1,0:T(8,128)(2,1)} %v_hbm.1) | copy-start | bytes 3145732
  5.8 0.9 %copy-start.3 = (f32[3,3,4096]{2,1,0:T(4,128)S(1)}, f32[3,3,4096]{2,1,0:T(4,128)}, u32[]{:S(2)}) copy-start(f32[3,3,4096]{2,1,0:T(4,128)} %taps_hbm.1) | copy-start | bytes 442372
  6.8 0.7 %copy-start.6 = (f32[2048]{0:T(1024)S(1)}, f32[2048]{0:T(1024)}, u32[]{:S(2)}) copy-start(f32[2048]{0:T(1024)} %param.13) | copy-start | bytes 24580

commit v3 on v2

--- a/solution.py
+++ b/solution.py
@@ -13,10 +13,10 @@
 
 def kernel(
     n, rows, chunks, width,
-    q_hbm, k_hbm, v_hbm, taps_hbm, decay_ref, lag_ref, skip_ref, keep_ref,
+    q_hbm, k_hbm, v_hbm, taps_hbm, decay_hbm, lag_hbm, skip_hbm, pairs_hbm,
     out_ref,
-    q_ref, k_ref, v_ref, taps_ref, rim_out, rim_in, gated, qfeat, spans, scaled, masked, toep,
-    outbox, inbox, start_acc, result, landed,
+    q_ref, k_ref, v_ref, taps_ref, decay_ref, lag_ref, skip_ref, pairs_ref, rim_out, rim_in, gated, qfeat, spans, scaled, masked, toep,
+    outbox, inbox, partial_sum, result, landed,
     load_sem, rim_sem, send1, recv1, send2, recv2, send_box, recv_box,
 ):
     me = lax.axis_index("ctx")
@@ -31,7 +31,11 @@
     loads = [
         pltpu.make_async_copy(src, dst, load_sem.at[index])
         for index, (src, dst) in enumerate(
-            ((k_hbm, k_ref), (v_hbm, v_ref), (taps_hbm, taps_ref), (q_hbm, q_ref))
+            (
+                (k_hbm, k_ref), (v_hbm, v_ref), (q_hbm, q_ref), (taps_hbm, taps_ref),
+                (lag_hbm, lag_ref), (decay_hbm, decay_ref), (skip_hbm, skip_ref),
+                (pairs_hbm, pairs_ref),
+            )
         )
     ]
     for load in loads:
@@ -52,22 +56,6 @@
         tail = ref[rows - 16 :, :].astype(jnp.float32)
         rim_out[2 * index : 2 * index + 2, :] = tail[14:16]
     rim_out[6:8, :] = jnp.zeros((2, rim_out.shape[1]), jnp.float32)
-
-    pl.semaphore_wait(barrier, n - 1)
-
-    def rim_copy(to):
-        return pltpu.make_async_remote_copy(
-            src_ref=rim_out, dst_ref=rim_in, send_sem=rim_sem.at[0], recv_sem=rim_sem.at[1],
-            device_id={"ctx": to}, device_id_type=MESH,
-        )
-
-    @pl.when(me < n - 1)
-    def _():
-        rim_copy(me + 1).start()
-
-    @pl.when(me == 0)
-    def _():
-        rim_in[...] = jnp.zeros_like(rim_in)
 
     def build(d, c):
         upper = lag_ref[:, pl.ds(pl.multiple_of(d * wide, wide), wide)]
@@ -78,6 +66,23 @@
         turned = pltpu.roll(window, 0, 1, stride=1, stride_axis=0)[:, :wide]
         toep[d] = turned.T.astype(jnp.bfloat16)
         return c
+
+    lax.fori_loop(0, n // 2, build, 0)
+    pl.semaphore_wait(barrier, n - 1)
+
+    def rim_copy(to):
+        return pltpu.make_async_remote_copy(
+            src_ref=rim_out, dst_ref=rim_in, send_sem=rim_sem.at[0], recv_sem=rim_sem.at[1],
+            device_id={"ctx": to}, device_id_type=MESH,
+        )
+
+    @pl.when(me < n - 1)
+    def _():
+        rim_copy(me + 1).start()
+
+    @pl.when(me == 0)
+    def _():
+        rim_in[...] = jnp.zeros_like(rim_in)
 
     @pl.when(me > 0)
     def _():
@@ -141,17 +146,17 @@
 
         lax.fori_loop(0, members, gate, 0)
 
-    lax.fori_loop(0, n // 2, build, 0)
-
     place = lax.broadcasted_iota(jnp.int32, (wide, width), 0).astype(jnp.float32)
 
     def rate_of(c):
         return decay_ref[:, columns(c, mine)]
 
+    listed = jnp.where(pairs_ref[:, 0, :] == 0, pairs_ref[:, 1, :], -1)
+    border = 1 + jnp.max(jnp.max(listed, axis=1, keepdims=True), axis=0, keepdims=True)
+    early = border <= members
+
     def keep_of(j):
-        return keep_ref[pl.ds(j, 1), 0:1]
-
-    early = keep_ref[n : n + 1, 0:1] > 0.5
+        return jnp.where(border == j, 0.0, 1.0)
 
     def matmul(a, b):
         return jnp.dot(a, b, preferred_element_type=jnp.float32)
@@ -186,33 +191,32 @@
             outbox[c, m] = jnp.where(early, source, acc).astype(jnp.bfloat16)
         box_copy(c, me + members).start()
 
+    def publish(c, i, top, bottom):
+        for side, value in enumerate((top, bottom)):
+            reader = 2 * i + side
+            value = value.astype(jnp.bfloat16)
+            result[c, reader] = value
+
+            @pl.when(reader != mine)
+            def _():
+                backward(c, reader, mine).start()
+
+            @pl.when(reader == mine)
+            def _():
+                landed[c, mine] = value
+
     def local(c):
         rate = rate_of(c)
         fade = jnp.exp(-rate * place)
         step_fade = jnp.exp(-rate * wide)
 
         def target(i, carry):
-            @pl.when(part == 0)
-            def _():
-                start_acc[...] = jnp.zeros_like(start_acc)
-
-            @pl.when(part == 1)
-            def _():
-                acc = matmul(toep[i + boxed], inbox[c, 0])
-                for m in range(1, boxed):
-                    span = 2 * (supers - boxed + m)
-                    both = keep_of(span) * keep_of(span + 1)
-                    acc = acc * (step_fade * both) + matmul(toep[i + boxed - m], inbox[c, m])
-                partial = inbox[c, jnp.minimum(i, boxed - 1)].astype(jnp.float32)
-                partial = jnp.where(i < boxed, partial, 0.0)
-                start_acc[...] = jnp.where(early, acc, partial)
-
             def source_step(j, acc):
                 span = base + 2 * j
                 both = keep_of(span) * keep_of(span + 1)
                 return acc * (step_fade * both) + matmul(toep[i - j], masked[c, j])
 
-            acc = lax.fori_loop(0, i, source_step, start_acc[...])
+            acc = lax.fori_loop(0, i, source_step, jnp.zeros((wide, width), jnp.float32))
             keep_first = keep_of(base + 2 * i)
             keep_second = keep_of(base + 2 * i + 1)
             top = acc[:rows] * (step_fade * keep_first) + matmul(
@@ -221,22 +225,47 @@
             bottom = acc[rows:] * (step_fade * keep_first * keep_second) + matmul(
                 toep[0, rows:wide, :], masked[c, i]
             )
-            for side, value in enumerate((top * fade[:rows], bottom * fade[rows:])):
-                reader = 2 * i + side
-                value = value.astype(jnp.bfloat16)
-                result[c, reader] = value
-
-                @pl.when(reader != mine)
-                def _():
-                    backward(c, reader, mine).start()
-
-                @pl.when(reader == mine)
-                def _():
-                    landed[c, mine] = value
+            top, bottom = top * fade[:rows], bottom * fade[rows:]
+
+            @pl.when(part == 0)
+            def _():
+                publish(c, i, top, bottom)
+
+            @pl.when(part == 1)
+            def _():
+                partial_sum[c, i, 0:rows, :] = top
+                partial_sum[c, i, rows:wide, :] = bottom
 
             return carry
 
         lax.fori_loop(0, supers, target, 0)
+
+    def join(c):
+        box_copy(c, me - members).wait_recv()
+        rate = rate_of(c)
+        step_fade = jnp.exp(-rate * wide)
+        fade = jnp.exp(-rate * (place + wide))
+
+        def target(i, far_fade):
+            acc = matmul(toep[i + boxed], inbox[c, 0])
+            for m in range(1, boxed):
+                span = 2 * (supers - boxed + m)
+                both = keep_of(span) * keep_of(span + 1)
+                acc = acc * (step_fade * both) + matmul(toep[i + boxed - m], inbox[c, m])
+            sent = inbox[c, jnp.minimum(i, boxed - 1)].astype(jnp.float32)
+            sent = jnp.where(i < boxed, sent, 0.0)
+            acc = jnp.where(early, acc, sent) * far_fade
+            last = base + 2 * i
+            live_top = jnp.where((border < base) | (border > last), 1.0, 0.0)
+            live_bottom = jnp.where((border < base) | (border > last + 1), 1.0, 0.0)
+            publish(
+                c, i,
+                partial_sum[c, i, 0:rows, :] + acc[:rows] * live_top,
+                partial_sum[c, i, rows:wide, :] + acc[rows:] * live_bottom,
+            )
+            return far_fade * step_fade
+
+        lax.fori_loop(0, supers, target, fade)
 
     for c in range(chunks):
         prepare(c)
@@ -244,6 +273,9 @@
         @pl.when(part == 0)
         def _():
             post(c)
+
+    for c in range(chunks):
+        local(c)
 
     def query(p, carry):
         for c in range(chunks):
@@ -256,9 +288,7 @@
 
         @pl.when(part == 1)
         def _():
-            box_copy(c, me - members).wait_recv()
-
-        local(c)
+            join(c)
 
     for c in range(chunks):
 
@@ -306,10 +336,7 @@
     share = channels // members
     width = min(CHUNK, max(128, share // 2))
     chunks = share // width
-    sources, targets = pair_lists[:, :, 0], pair_lists[:, :, 1]
-    border = 1 + jnp.max(jnp.where(sources == 0, targets, -1))
-    index = lax.broadcasted_iota(jnp.int32, (n + 8, 128), 0)
-    keep = jnp.where(index == n, border <= members, index != border).astype(jnp.float32)
+    pairs = pair_lists.transpose(1, 2, 0)
     vmem = pl.BlockSpec(memory_space=pltpu.VMEM)
     hbm = pl.BlockSpec(memory_space=pltpu.HBM)
     bf16, f32 = jnp.bfloat16, jnp.float32
@@ -318,13 +345,17 @@
     return pl.pallas_call(
         functools.partial(kernel, n, rows, chunks, width),
         out_shape=jax.ShapeDtypeStruct((rows, channels), bf16),
-        in_specs=[hbm] * 4 + [vmem] * 4,
+        in_specs=[hbm] * 8,
         out_specs=vmem,
         scratch_shapes=[
             pltpu.VMEM((rows, channels), bf16),
             pltpu.VMEM((rows, channels), bf16),
             pltpu.VMEM((rows, channels), bf16),
             pltpu.VMEM(conv_taps.shape, f32),
+            pltpu.VMEM((1, channels), f32),
+            pltpu.VMEM((1, lag_profile.shape[0]), f32),
+            pltpu.VMEM((1, channels), f32),
+            pltpu.VMEM(pairs.shape, jnp.int32),
             pltpu.VMEM((8, channels), f32),
             pltpu.VMEM((8, channels), f32),
             pltpu.VMEM(piece, bf16),
@@ -335,10 +366,10 @@
             pltpu.VMEM((n // 2, wide, wide), bf16),
             pltpu.VMEM((chunks, boxed, wide, width), bf16),
             pltpu.VMEM((chunks, boxed, wide, width), bf16),
-            pltpu.VMEM((wide, width), f32),
+            pltpu.VMEM((chunks, supers, wide, width), f32),
             pltpu.VMEM(piece, bf16),
             pltpu.VMEM(piece, bf16),
-            dma((4,)),
+            dma((8,)),
             dma((2,)),
             dma((chunks, members)),
             dma((chunks, members)),
@@ -348,11 +379,11 @@
             dma((chunks,)),
         ],
         compiler_params=pltpu.CompilerParams(
-            collective_id=0, has_side_effects=True, vmem_limit_bytes=48 * 1024 * 1024
+            collective_id=0, has_side_effects=True, vmem_limit_bytes=62 * 1024 * 1024
         ),
     )(
         query_rows, key_rows, value_rows, conv_taps, decay_rate.reshape(1, -1),
-        lag_profile.reshape(1, -1), skip_gain.reshape(1, -1), keep,
+        lag_profile.reshape(1, -1), skip_gain.reshape(1, -1), pairs,
     )
 
 

time: 60.2 us -> 52.9 us (0.88)
  local copies, waits for them, and re-layouts: 6.35 us -> 2.29 us
  other arithmetic: 1.43 us -> 0 us
  Pallas kernels: 51.4 us -> 50.4 us
  between operations: 0.68 us -> 0.01 us
    unnamed x15 -> x1, local copies, waits for them, and re-layouts: 6.28 us -> 2.29 us
    reduce_max x1 -> x0, other arithmetic: 1.42 us -> none  [on_device(): border = 1 + jnp.max(jnp.where(sources == 0, targets, -1))]
    pallas_call x1, Pallas kernels: 51.4 us -> 50.4 us  [on_device(): pl.pallas_call(functools.partial(kernel, n, rows, chunks, width), out_sha...]
where the time goes in v3:
time: 52.9 us; the launch traced here: 52.7 us
  Pallas kernels  50.4 us (95%)
  local copies, waits for them, and re-layouts  2.29 us (4%)
    pallas_call x1, Pallas kernels, on_device(): pl.pallas_call(functools.partial(kernel, n, rows, chunks, width), out_sha...  50.4 us
    unnamed x1, local copies, waits for them, and re-layouts  2.29 us

profile of v3, /device:TPU:29, one launch (start us, length us, event | category | flops | bytes accessed | tf_op | source)
XLA Modules:
  0.0 52.7 jit_solution(8214998808263084902)
XLA Ops:
  0.0 50.4 %shard_map.82 = bf16[128,4096]{1,0:T(8,128)(2,1)} custom-call(bf16[128,4096]{1,0:T(8,128)(2,1)} %q_hbm.1, bf16[128,4096]{1,0:T(8,128)(2,1)} %k_hbm.1, bf16[128,4096]{1,0:T(8,128)(2,1)} %v_hbm.1, f32[3,3,4096]{2,1,0:T(4,128)} %taps_hbm.1, f32[1,4096]{1,0:T(1,128)} %bitcast.4, f32[1,2048]{1,0:T(1,128)} %bitcast.7, f32[1,4096]{1,0:T(1,128)} %bitcast.5, ...), custom_call_target="tpu_custom_call" | custom-call | tf_op jit(solution)/shard_map/pallas_call | solution.py:345
  50.4 2.3 %copy.10 = bf16[128,4096]{1,0:T(8,128)(2,1)} copy(bf16[128,4096]{1,0:T(8,128)(2,1)} %shard_map.82) | data formatting | bytes 2097152

commit v4 on v3

--- a/solution.py
+++ b/solution.py
@@ -8,7 +8,7 @@
 from jax.sharding import PartitionSpec as P
 
 MESH = pl.DeviceIdType.MESH
-CHUNK = 256
+CHUNK = 128
 
 
 def kernel(
@@ -126,16 +126,17 @@
             device_id={"ctx": to}, device_id_type=MESH,
         )
 
-    for c in range(chunks):
-
-        def gate(k, carry, c=c):
-            p = lax.rem(mine + members // 2 + k, members)
+    def gate_chunk(c):
+        def gate(k, carry):
+            p = lax.rem(mine + 1 + k, members)
             cols = columns(c, p)
             value = (feature(k_ref, 1, cols) * feature(v_ref, 2, cols)).astype(jnp.bfloat16)
             gated[c, p] = value
 
             @pl.when(p != mine)
             def _():
+                if c > 0:
+                    forward(c - 1, p, mine).wait_send()
                 forward(c, p, mine).start()
 
             @pl.when(p == mine)
@@ -267,7 +268,10 @@
 
         lax.fori_loop(0, supers, target, fade)
 
+    gate_chunk(0)
     for c in range(chunks):
+        if c + 1 < chunks:
+            gate_chunk(c + 1)
         prepare(c)
 
         @pl.when(part == 0)
@@ -275,6 +279,7 @@
             post(c)
 
     for c in range(chunks):
+
         local(c)
 
     def query(p, carry):
@@ -310,8 +315,8 @@
 
     def drain(k, carry):
         p = lax.rem(mine + k, members)
+        forward(chunks - 1, p, mine).wait_send()
         for c in range(chunks):
-            forward(c, p, mine).wait_send()
             backward(c, p, mine).wait_send()
         return carry
 

time: 52.9 us -> 51.3 us (0.970)
  Pallas kernels: 50.4 us -> 48.8 us
    pallas_call x1, Pallas kernels: 50.4 us -> 48.8 us  [on_device(): pl.pallas_call(functools.partial(kernel, n, rows, chunks, width), out_sha...]
where the time goes in v4:
time: 51.3 us; the launch traced here: 51.1 us
  Pallas kernels  48.8 us (95%)
  local copies, waits for them, and re-layouts  2.29 us (4%)
    pallas_call x1, Pallas kernels, on_device(): pl.pallas_call(functools.partial(kernel, n, rows, chunks, width), out_sha...  48.8 us
    unnamed x1, local copies, waits for them, and re-layouts  2.29 us

profile of v4, /device:TPU:29, one launch (start us, length us, event | category | flops | bytes accessed | tf_op | source)
XLA Modules:
  0.0 51.1 jit_solution(14008514768583699509)
XLA Ops:
  0.0 48.8 %shard_map.82 = bf16[128,4096]{1,0:T(8,128)(2,1)} custom-call(bf16[128,4096]{1,0:T(8,128)(2,1)} %q_hbm.1, bf16[128,4096]{1,0:T(8,128)(2,1)} %k_hbm.1, bf16[128,4096]{1,0:T(8,128)(2,1)} %v_hbm.1, f32[3,3,4096]{2,1,0:T(4,128)} %taps_hbm.1, f32[1,4096]{1,0:T(1,128)} %bitcast.4, f32[1,2048]{1,0:T(1,128)} %bitcast.7, f32[1,4096]{1,0:T(1,128)} %bitcast.5, ...), custom_call_target="tpu_custom_call" | custom-call | tf_op jit(solution)/shard_map/pallas_call | solution.py:350
  48.8 2.3 %copy.10 = bf16[128,4096]{1,0:T(8,128)(2,1)} copy(bf16[128,4096]{1,0:T(8,128)(2,1)} %shard_map.82) | data formatting | bytes 2097152

commit v5 on v4

--- a/solution.py
+++ b/solution.py
@@ -9,15 +9,16 @@
 
 MESH = pl.DeviceIdType.MESH
 CHUNK = 128
+STRIPS = 8
 
 
 def kernel(
     n, rows, chunks, width,
     q_hbm, k_hbm, v_hbm, taps_hbm, decay_hbm, lag_hbm, skip_hbm, pairs_hbm,
-    out_ref,
-    q_ref, k_ref, v_ref, taps_ref, decay_ref, lag_ref, skip_ref, pairs_ref, rim_out, rim_in, gated, qfeat, spans, scaled, masked, toep,
+    out_hbm,
+    out_ref, q_ref, k_ref, v_ref, taps_ref, decay_ref, lag_ref, skip_ref, pairs_ref, rim_out, rim_in, gated, qfeat, spans, scaled, masked, toep,
     outbox, inbox, partial_sum, result, landed,
-    load_sem, rim_sem, send1, recv1, send2, recv2, send_box, recv_box,
+    load_sem, store_sem, rim_sem, send1, recv1, send2, recv2, send_box, recv_box,
 ):
     me = lax.axis_index("ctx")
     wide = 2 * rows
@@ -295,6 +296,10 @@
         def _():
             join(c)
 
+    def store(c, p):
+        cols = columns(c, p)
+        return pltpu.make_async_copy(out_ref.at[:, cols], out_hbm.at[:, cols], store_sem.at[c, p])
+
     for c in range(chunks):
 
         def finish(k, carry, c=c):
@@ -309,6 +314,7 @@
             out_ref[:, cols] = (
                 qfeat[c, p] * (landed[c, p].astype(jnp.float32) + direct)
             ).astype(jnp.bfloat16)
+            store(c, p).start()
             return carry
 
         lax.fori_loop(0, members, finish, 0)
@@ -322,6 +328,13 @@
 
     lax.fori_loop(1, members, drain, 0)
 
+    def stored(p, carry):
+        for c in range(chunks):
+            store(c, p).wait()
+        return carry
+
+    lax.fori_loop(0, members, stored, 0)
+
     @pl.when(part == 0)
     def _():
         for c in range(chunks):
@@ -330,6 +343,24 @@
     @pl.when(me < n - 1)
     def _():
         rim_copy(me + 1).wait_send()
+
+
+def hand_over(strip, src_ref, dst_ref, held, in_sem, out_sem):
+    def load(i):
+        part = pl.ds(i * strip, strip)
+        return pltpu.make_async_copy(src_ref.at[part], held.at[part], in_sem.at[i])
+
+    def store(i):
+        part = pl.ds(i * strip, strip)
+        return pltpu.make_async_copy(held.at[part], dst_ref.at[part], out_sem.at[i])
+
+    for i in range(STRIPS):
+        load(i).start()
+    for i in range(STRIPS):
+        load(i).wait()
+        store(i).start()
+    for i in range(STRIPS):
+        store(i).wait()
 
 
 def on_device(
@@ -342,17 +373,17 @@
     width = min(CHUNK, max(128, share // 2))
     chunks = share // width
     pairs = pair_lists.transpose(1, 2, 0)
-    vmem = pl.BlockSpec(memory_space=pltpu.VMEM)
     hbm = pl.BlockSpec(memory_space=pltpu.HBM)
     bf16, f32 = jnp.bfloat16, jnp.float32
     piece = (chunks, members, rows, width)
     dma = pltpu.SemaphoreType.DMA
-    return pl.pallas_call(
+    held = pl.pallas_call(
         functools.partial(kernel, n, rows, chunks, width),
         out_shape=jax.ShapeDtypeStruct((rows, channels), bf16),
         in_specs=[hbm] * 8,
-        out_specs=vmem,
+        out_specs=hbm,
         scratch_shapes=[
+            pltpu.VMEM((rows, channels), bf16),
             pltpu.VMEM((rows, channels), bf16),
             pltpu.VMEM((rows, channels), bf16),
             pltpu.VMEM((rows, channels), bf16),
@@ -375,6 +406,7 @@
             pltpu.VMEM(piece, bf16),
             pltpu.VMEM(piece, bf16),
             dma((8,)),
+            dma((chunks, members)),
             dma((2,)),
             dma((chunks, members)),
             dma((chunks, members)),
@@ -390,6 +422,14 @@
         query_rows, key_rows, value_rows, conv_taps, decay_rate.reshape(1, -1),
         lag_profile.reshape(1, -1), skip_gain.reshape(1, -1), pairs,
     )
+    return pl.pallas_call(
+        functools.partial(hand_over, rows // STRIPS),
+        out_shape=jax.ShapeDtypeStruct((rows, channels), bf16),
+        in_specs=[hbm],
+        out_specs=hbm,
+        scratch_shapes=[pltpu.VMEM((rows, channels), bf16), dma((STRIPS,)), dma((STRIPS,))],
+        compiler_params=pltpu.CompilerParams(vmem_limit_bytes=62 * 1024 * 1024),
+    )(held)
 
 
 def solution(mesh):

time: 51.3 us -> 50.9 us (level)
  local copies, waits for them, and re-layouts: 2.29 us -> 0 us
  Pallas kernels: 48.8 us -> 50.7 us
    unnamed x1 -> x0, local copies, waits for them, and re-layouts: 2.29 us -> none
    pallas_call x0 -> x1, Pallas kernels: none -> 2.09 us  [on_device(): pl.pallas_call(functools.partial(hand_over, rows // STRIPS), out_shape=ja...]
where the time goes in v5:
time: 50.9 us; the launch traced here: 50.7 us
  Pallas kernels  50.7 us (100%)
    pallas_call x1, Pallas kernels, on_device(): pl.pallas_call(functools.partial(kernel, n, rows, chunks, width), out_sha...  48.6 us
    pallas_call x1, Pallas kernels, on_device(): pl.pallas_call(functools.partial(hand_over, rows // STRIPS), out_shape=ja...  2.09 us

profile of v5, /device:TPU:29, one launch (start us, length us, event | category | flops | bytes accessed | tf_op | source)
XLA Modules:
  0.0 50.7 jit_solution(424856470643108457)
XLA Ops:
  0.0 48.6 %shard_map.82.src_ref = bf16[128,4096]{1,0:T(8,128)(2,1)} custom-call(bf16[128,4096]{1,0:T(8,128)(2,1)} %q_hbm.1, bf16[128,4096]{1,0:T(8,128)(2,1)} %k_hbm.1, bf16[128,4096]{1,0:T(8,128)(2,1)} %v_hbm.1, f32[3,3,4096]{2,1,0:T(4,128)} %taps_hbm.1, f32[1,4096]{1,0:T(1,128)} %bitcast.4, f32[1,2048]{1,0:T(1,128)} %bitcast.7, f32[1,4096]{1,0:T(1,128)} %bitcast.5, ...), custom_call_target="tpu_custom_call" | custom-call | tf_op jit(solution)/shard_map/pallas_call | solution.py:380
  48.6 2.1 %shard_map.83 = bf16[128,4096]{1,0:T(8,128)(2,1)} custom-call(bf16[128,4096]{1,0:T(8,128)(2,1)} %shard_map.82.src_ref), custom_call_target="tpu_custom_call" | custom-call | tf_op jit(solution)/shard_map/pallas_call | solution.py:425
